TPU v7x, 512 devices: a whole 4x4x16 slice. The times are simulated.
512 devices in a mesh: replica: 64 (over x_lo, z, core), tensor: 8 (over x_hi, y).
Axes of the slice: x: 4 (x_hi: 2, x_lo: 2; x = x_hi * 2 + x_lo), y: 4, z: 16, core: 2. Of those that a mesh axis runs over, the one named last changes fastest.
Arguments:
- qkv_weight: bfloat16 [5120, 7168], P(('replica', 'tensor')), may hold values from -0.078125 to 0.078125
- qkv_bias: bfloat16 [7168], P('tensor'), may hold values from -7 to 7
- norm_gain: bfloat16 [5120], replicated, may hold values from 0.099609375 to 1.8984375
- decode_hidden: bfloat16 [1024, 5120], P('replica'), may hold values from -6 to 6
- stored_keys: bfloat16 [1024, 8, 256, 128], P('replica', 'tensor'), may hold values from -72 to 72
- stored_values: bfloat16 [1024, 8, 256, 128], P('replica', 'tensor'), may hold values from -6 to 6
- stored_lengths: int32 [64, 16], P('replica'), may hold values from 1 to 256, 2048 in all within a row
- response_hidden: bfloat16 [640, 64, 5120], P('replica', None, 'tensor'), may hold values from -6 to 6
- response_lengths: int32 [64, 10], P('replica'), may hold values from 1 to 64, 560 in all within a row
- response_target: int32 [640, 1], P('replica'), may hold values from 0 to 7; in each aligned block of 10 rows (0 to 9, 10 to 19, ...) at most 2 rows name the same one
Outputs:
- step_attention: bfloat16 [1024, 5120], P('replica', 'tensor')
- learner_attention: bfloat16 [1024, 64, 5120], P(('replica', 'tensor'))
Inputs may be any that keep to these rules, and one draw needn't show every extreme that they name: `response_lengths`: the 10 lengths of one group sum to 560, and one of them equals 64. `stored_lengths`: the 16 lengths of one group sum to 2048, and one of them equals 256. `response_target`: among the 10 responses of one rollout group at most 2 name the same learner device, and in some groups one device is named by exactly 2.
All inputs are finite; a program needn't handle non-finite values.
Results may differ from a plain program's by a relative error of at most 0.0065.
The roundings to bfloat16 on the way count: a program that leaves them out, or rounds other values in their place, can miss the bound.
Values may be sent and summed in bfloat16 or wider, within the bound.
A program may use at most 64 MiB of HBM per device.

v0:
```python
import math

import jax
import jax.numpy as jnp
from jax import lax
from jax.sharding import PartitionSpec as P

MODEL_WIDTH = 5120
QUERY_HEADS = 40
KV_HEADS = 8
HEAD_DIM = 128
DONE_PER_GROUP = 10
RESPONSE_LIMIT = 64


def normalize(rows_in, gain_vec):
    widened = rows_in.astype(jnp.float32)
    inverse = lax.rsqrt(jnp.mean(widened * widened, axis=-1, keepdims=True) + 1e-06)
    return (widened * inverse * gain_vec.astype(jnp.float32)).astype(jnp.bfloat16)


def block_attend(qkv_rows, token_lengths):
    rollout_groups = qkv_rows.shape[3] - 2
    head_size = qkv_rows.shape[4]
    number = qkv_rows.shape[0]
    length = qkv_rows.shape[1]
    query = qkv_rows[:, :, :, :rollout_groups]
    key_matrix = qkv_rows[:, :, :, rollout_groups]
    value_matrix = qkv_rows[:, :, :, rollout_groups + 1]
    scores = jnp.einsum(
        "nikgh,njkh->nkgij", query, key_matrix, preferred_element_type=jnp.float32
    ) / math.sqrt(head_size)
    causal = jnp.arange(length)[None, :] <= jnp.arange(length)[:, None]
    masked = jnp.where(causal, scores, -jnp.inf)
    peak = jnp.max(masked, axis=-1, keepdims=True)
    powers = jnp.where(causal, jnp.exp(scores - peak), 0.0)
    probs = (powers / jnp.sum(powers, axis=-1, keepdims=True)).astype(jnp.bfloat16)
    mixture = jnp.einsum(
        "nkgij,njkh->nikgh", probs, value_matrix, preferred_element_type=jnp.float32
    )
    in_range = jnp.arange(length)[None, :] < token_lengths[:, None]
    mixture = jnp.where(in_range[:, :, None, None, None], mixture, 0.0)
    return mixture.astype(jnp.bfloat16).reshape(number, length, -1)


def attend_decoding(qkv_rows, key_cache, value_cache, token_lengths):
    rollout_groups = qkv_rows.shape[2] - 2
    head_size = qkv_rows.shape[3]
    number = qkv_rows.shape[0]
    query = qkv_rows[:, :, :rollout_groups]
    new_key = qkv_rows[:, :, rollout_groups]
    new_value = qkv_rows[:, :, rollout_groups + 1]
    scores = jnp.einsum(
        "bkgh,bklh->bkgl", query, key_cache, preferred_element_type=jnp.float32
    ) / math.sqrt(head_size)
    self_score = jnp.einsum("bkgh,bkh->bkg", query, new_key, preferred_element_type=jnp.float32)[
        ..., None
    ] / math.sqrt(head_size)
    filled = (jnp.arange(key_cache.shape[2])[None, :] < token_lengths[:, None])[:, None, None, :]
    peak = jnp.maximum(
        jnp.max(jnp.where(filled, scores, -jnp.inf), axis=-1, keepdims=True), self_score
    )
    powers = jnp.where(filled, jnp.exp(scores - peak), 0.0)
    self_power = jnp.exp(self_score - peak)
    total = jnp.sum(powers, axis=-1, keepdims=True) + self_power
    probs = (powers / total).astype(jnp.bfloat16)
    self_prob = (self_power / total).astype(jnp.bfloat16)
    mixture = jnp.einsum("bkgl,bklh->bkgh", probs, value_cache, preferred_element_type=jnp.float32)
    mixture = mixture + self_prob.astype(jnp.float32) * new_value.astype(jnp.float32)[:, :, None, :]
    return mixture.astype(jnp.bfloat16).reshape(number, -1)


def selector(targets, shards, slot_capacity):
    number = targets.shape[0]
    same_dest = targets[:, None] == targets[None, :]
    earlier = jnp.arange(number)[None, :] < jnp.arange(number)[:, None]
    slot_index = jnp.sum((same_dest & earlier).astype(jnp.int32), axis=1)
    target_slot = targets * slot_capacity + slot_index
    return (
        jnp.arange(shards * slot_capacity, dtype=jnp.int32)[:, None] == target_slot[None, :]
    ).astype(jnp.int32)


def body(
    qkv_weight,
    qkv_bias,
    norm_gain,
    decode_hidden,
    stored_keys,
    stored_values,
    stored_lengths,
    response_hidden,
    response_lengths,
    response_target,
):
    tensor_count = lax.axis_size("tensor")
    rollout_groups = QUERY_HEADS // KV_HEADS
    slot_capacity = DONE_PER_GROUP // tensor_count + 1
    rows_local = qkv_weight.shape[0]
    col_width = qkv_weight.shape[1] // tensor_count
    local_groups = col_width // ((rollout_groups + 2) * HEAD_DIM)
    blocks = lax.all_to_all(
        qkv_weight.reshape(rows_local, tensor_count, col_width),
        "tensor",
        split_axis=1,
        concat_axis=0,
        tiled=True,
    )
    blocks = blocks.reshape(rows_local * tensor_count, col_width)
    step_norm = normalize(decode_hidden, norm_gain)
    resp_full = lax.all_gather(response_hidden, "tensor", axis=2, tiled=True)
    resp_norm = normalize(resp_full, norm_gain).reshape(
        DONE_PER_GROUP * RESPONSE_LIMIT, MODEL_WIDTH
    )
    weight_all = lax.all_gather(blocks, "replica", axis=0, tiled=True)
    step_acc = jnp.dot(step_norm, weight_all, preferred_element_type=jnp.float32)
    resp_acc = jnp.dot(resp_norm, weight_all, preferred_element_type=jnp.float32)
    offset = qkv_bias.astype(jnp.float32)
    decode_projected = (
        (step_acc + offset)
        .astype(jnp.bfloat16)
        .reshape(-1, local_groups, rollout_groups + 2, HEAD_DIM)
    )
    response_projected = (
        (resp_acc + offset).astype(jnp.bfloat16).reshape(DONE_PER_GROUP, RESPONSE_LIMIT, col_width)
    )
    decode_output = attend_decoding(
        decode_projected, stored_keys, stored_values, stored_lengths.reshape(-1)
    )
    token_lengths = response_lengths.reshape(DONE_PER_GROUP)
    targets = response_target.reshape(DONE_PER_GROUP)
    chooser = selector(targets, tensor_count, slot_capacity)
    mine = lax.dynamic_slice_in_dim(
        chooser, lax.axis_index("tensor") * slot_capacity, slot_capacity, 0
    )
    slot_lens = jnp.sum(mine * token_lengths[None, :], axis=1)
    chooser_cube = chooser.astype(jnp.bfloat16).reshape(tensor_count, slot_capacity, DONE_PER_GROUP)
    sendbuf = jnp.einsum(
        "dcj,jrw->crdw", chooser_cube, response_projected, preferred_element_type=jnp.float32
    ).astype(jnp.bfloat16)
    received_rows = lax.all_to_all(sendbuf, "tensor", split_axis=2, concat_axis=2, tiled=True)
    received_rows = received_rows.reshape(
        slot_capacity, RESPONSE_LIMIT, KV_HEADS, rollout_groups + 2, HEAD_DIM
    )
    learner_out = block_attend(received_rows, slot_lens)
    return (decode_output, learner_out)


def solution(mesh):
    return jax.shard_map(
        body,
        mesh=mesh,
        in_specs=(
            P(("replica", "tensor"), None),
            P("tensor"),
            P(),
            P("replica", None),
            P("replica", "tensor", None, None),
            P("replica", "tensor", None, None),
            P("replica", None),
            P("replica", None, "tensor"),
            P("replica", None),
            P("replica", None),
        ),
        out_specs=(P("replica", "tensor"), P(("replica", "tensor"), None, None)),
        check_vma=False,
    )
```

profile of v0, /device:TPU:1, one launch (start us, length us, event | category | flops | bytes accessed | tf_op | source)
XLA Modules:
  0.0 312.3 jit_solution(8639920904462327456)
XLA Ops:
  7.3 0.7 all-gather.5.cloned.1.call-update
  8.0 1.0 copy.58
  9.0 14.8 %all_to_all.20 = bf16[10,8,896]{2,0,1:T(8,128)(2,1)S(1)} all-to-all(bf16[10,8,896]{2,0,1:T(8,128)(2,1)S(1)} %copy.38), channel_id=1, replica_groups=mesh['replica'=64,'tensor'=8] {'tensor'}, dimensions={1} | all-to-all | bytes 286720 | tf_op jit(solution)/shard_map/all_to_all | solution.py:102
  23.8 0.7 reshape.186
  25.3 96.4 %all-gather.5.cloned.1.call-done = bf16[10,64,5120]{2,1,0:T(8,128)(2,1)} async-done(((bf16[10,64,640]{2,1,0:T(8,128)(2,1)}), bf16[10,64,5120]{2,1,0:T(8,128)(2,1)}) %all-gather.5.cloned.1.call-update) | async-done | bytes 6553616 | tf_op jit(solution)/shard_map/all_gather | solution.py:111
  121.7 4.4 %fusion.1 = f32[10,64]{1,0:T(8,128)S(1)} fusion(bf16[10,64,5120]{2,1,0:T(8,128)(2,1)} %all-gather.5.cloned.1.call-done), kind=kLoop, calls=%fused_computation.3 | loop fusion | flops 9829760 | bytes 6556160 | tf_op jit(solution)/shard_map/reduce_sum | solution.py:18
  126.1 0.4 copy-done.1
  126.4 5.3 %fusion.3 = bf16[10,64,5120]{2,1,0:T(8,128)(2,1)} fusion(bf16[10,64,5120]{2,1,0:T(8,128)(2,1)S(1)} %copy-done.1, f32[5120]{0:T(1024)S(1)} %convert_element_type.82, f32[10,64]{1,0:T(8,128)S(1)} %add_rsqrt_fusion), kind=kLoop, calls=%fused_computation.5 | loop fusion | flops 13107200 | bytes 13130240 | tf_op jit(solution)/shard_map/convert_element_type | solution.py:19
  131.7 121.0 %all-gather.3.cloned.1.call-done = bf16[5120,896]{1,0:T(8,128)(2,1)} async-done(((bf16[80,896]{1,0:T(8,128)(2,1)}), bf16[5120,896]{1,0:T(8,128)(2,1)}) %all-gather.3.cloned.1.call-update) | async-done | bytes 9175056 | tf_op jit(solution)/shard_map/all_gather | solution.py:115
  252.8 11.8 %add_convert_fusion = bf16[640,896]{1,0:T(8,128)(2,1)S(1)} fusion(bf16[640,5120]{1,0:T(8,128)(2,1)} %bitcast.81, bf16[5120,896]{1,0:T(8,128)(2,1)} %all-gather.3.cloned.1.call-done, f32[896]{0:T(1024)S(1)} %convert_element_type.84), kind=kOutput, calls=%fused_computation.14 | convolution fusion | flops 5873172480 | bytes 16879104 | tf_op jit(solution)/shard_map/dot_general | solution.py:117
  264.5 0.9 convert_bitcast_fusion
  265.5 2.7 copy.40
  268.1 6.4 %all-to-all-start.1 = ((bf16[2,64,8,896]{3,0,1,2:T(2,128)(2,1)}), bf16[2,64,8,896]{3,0,1,2:T(2,128)(2,1)S(1)}, u32[]{:S(2)}, u32[]{:S(2)}) async-start(bf16[2,64,8,896]{3,0,1,2:T(2,128)(2,1)} %copy.40), calls=%async_computation.1 | async-start | bytes 3670016 | tf_op jit(solution)/shard_map/all_to_all | solution.py:141
  274.6 4.9 %fusion.19 = bf16[16,896]{1,0:T(8,128)(2,1)S(1)} fusion(bf16[5120,896]{1,0:T(8,128)(2,1)} %all-gather.3.cloned.1.call-done, bf16[16,5120]{1,0:T(8,128)(2,1)S(1)} %copy-done.2, f32[5120]{0:T(1024)S(1)} %convert_element_type.82, f32[16]{0:T(128)S(1)} %add_rsqrt_fusion.1, f32[896]{0:T(1024)S(1)} %convert_element_type.84), kind=kOutput, calls=%fused_computation.29 | convolution fusion | flops 147156992 | bytes 9391680 | tf_op jit(solution)/shard_map/dot_general | solution.py:116
  279.7 0.5 select_reduce_fusion
  280.4 1.5 fusion.18
  281.9 0.6 copy.73
  282.6 15.4 %all-to-all-done.1 = bf16[2,64,8,896]{3,0,1,2:T(2,128)(2,1)S(1)} async-done(((bf16[2,64,8,896]{3,0,1,2:T(2,128)(2,1)}), bf16[2,64,8,896]{3,0,1,2:T(2,128)(2,1)S(1)}, u32[]{:S(2)}, u32[]{:S(2)}) %all-to-all-start.1) | async-done | bytes 1835040 | tf_op jit(solution)/shard_map/all_to_all | solution.py:141
  298.0 1.0 copy.72
  299.2 1.2 fusion.13
  300.4 1.0 fusion.47
  301.4 0.8 fusion.12
  302.2 0.9 copy.46
  303.2 2.3 reshape.197
  (40 shorter events, 1.4 us)
Async XLA Ops:
  7.2 272.5 %copy-start = (bf16[16,1,256,128]{3,2,1,0:T(8,128)(2,1)S(1)}, bf16[16,1,256,128]{3,2,1,0:T(8,128)(2,1)}, u32[]{:S(2)}) copy-start(bf16[16,1,256,128]{3,2,1,0:T(8,128)(2,1)} %param.14) | copy-start | bytes 3145732
  7.2 17.4 %copy-start.4 = (bf16[896]{0:T(1024)(128)(2,1)S(1)}, bf16[896]{0:T(1024)(128)(2,1)}, u32[]{:S(2)}) copy-start(bf16[896]{0:T(1024)(128)(2,1)} %param.11) | copy-start | bytes 5380
  7.2 17.4 %copy-start.3 = (bf16[5120]{0:T(1024)(128)(2,1)S(1)}, bf16[5120]{0:T(1024)(128)(2,1)}, u32[]{:S(2)}) copy-start(bf16[5120]{0:T(1024)(128)(2,1)} %param.12) | copy-start | bytes 30724
  7.2 17.4 %copy-start.7 = (s32[10,1]{0,1:T(1,128)S(1)}, s32[10,1]{0,1:T(1,128)}, u32[]{:S(2)}) copy-start(s32[10,1]{0,1:T(1,128)} %param.19) | copy-start | bytes 124
  7.2 17.6 %copy-start.6 = (s32[1,10]{1,0:T(1,128)S(1)}, s32[1,10]{1,0:T(1,128)}, u32[]{:S(2)}) copy-start(s32[1,10]{1,0:T(1,128)} %param.18) | copy-start | bytes 124
  7.2 17.7 %copy-start.2 = (bf16[16,5120]{1,0:T(8,128)(2,1)S(1)}, bf16[16,5120]{1,0:T(8,128)(2,1)}, u32[]{:S(2)}) copy-start(bf16[16,5120]{1,0:T(8,128)(2,1)} %param.13) | copy-start | bytes 491524
  7.2 18.0 %copy-start.5 = (s32[1,16]{1,0:T(1,128)S(1)}, s32[1,16]{1,0:T(1,128)}, u32[]{:S(2)}) copy-start(s32[1,16]{1,0:T(1,128)} %param.16) | copy-start | bytes 196
  7.2 114.5 %all-gather.5.cloned.1.call-start = ((), (), s32[]{:S(2)}) async-start(), calls=%async_computation.3 | async-start | bytes 7372800 | tf_op jit(solution)/shard_map/all_gather | solution.py:111
  8.0 244.8 %all-gather.3.cloned.1.call-start = ((), (), s32[]{:S(2)}) async-start(), calls=%async_computation.2 | async-start | bytes 9318400 | tf_op jit(solution)/shard_map/all_gather | solution.py:115
  121.7 4.7 %copy-start.1 = (bf16[10,64,5120]{2,1,0:T(8,128)(2,1)S(1)}, bf16[10,64,5120]{2,1,0:T(8,128)(2,1)}, u32[]{:S(2)}) copy-start(bf16[10,64,5120]{2,1,0:T(8,128)(2,1)} %all-gather.5.cloned.1.call-done) | copy-start | bytes 19660804
  268.1 29.8 %all-to-all-start.1 = ((bf16[2,64,8,896]{3,0,1,2:T(2,128)(2,1)}), bf16[2,64,8,896]{3,0,1,2:T(2,128)(2,1)S(1)}, u32[]{:S(2)}, u32[]{:S(2)}) async-start(bf16[2,64,8,896]{3,0,1,2:T(2,128)(2,1)} %copy.40), calls=%async_computation.1 | async-start | bytes 3670016 | tf_op jit(solution)/shard_map/all_to_all | solution.py:141
Sparse Core Ops, SparseCore 0:
  11.3 110.3 all-gather.4
  124.4 128.2 all-gather.2
where the time goes:
time: 313 us; the launch traced here: 312 us
  waiting for transfers between devices  234 us (75%)
  matrix products  21.8 us (7%)
  blocking collectives  14.8 us (5%)
  between operations  14.3 us (5%)
  other arithmetic  11.5 us (4%)
  local copies, waits for them, and re-layouts  9.97 us (3%)
  starting transfers between devices  6.51 us (2%)
    all_gather x1, waiting for transfers between devices, body(): weight_all = lax.all_gather(blocks, 'replica', axis=0, tiled=True)  121 us
    all_gather x1, waiting for transfers between devices, body(): resp_full = lax.all_gather(response_hidden, 'tensor', axis=2, tiled=True)  96.4 us
    all_to_all x1, waiting for transfers between devices, body(): lax.all_to_all(sendbuf, 'tensor', split_axis=2, concat_axis=2, tiled=True)  15.4 us
    all_to_all x1, blocking collectives, body(): lax.all_to_all(qkv_weight.reshape(rows_local, tensor_count, col_width), '...  14.8 us
    dot_general x1, matrix products, body(): jnp.dot(resp_norm, weight_all, preferred_element_type=jnp.float32)  11.8 us
    all_to_all x1, starting transfers between devices, body(): lax.all_to_all(sendbuf, 'tensor', split_axis=2, concat_axis=2, tiled=True)  6.43 us
  transfers between devices with their start and end apart: 3, of which 3 were waited for; matrix products, arithmetic and copies ran while one was open for 6% of the time, Pallas kernels for 0%

commit v1 on v0

v1 whole, which is shorter than its diff:
```python
import math

import jax
import jax.numpy as jnp
from jax import lax
from jax.experimental import pallas as pl
from jax.experimental.pallas import tpu as pltpu
from jax.sharding import PartitionSpec as P

MODEL_WIDTH = 5120
HEADS = 5
HEAD_DIM = 128
DONE = 10
LIMIT = 64
LIVE = 560
STEPS = 16
CACHE = 256
COLS = 896
FEAT = 640
OUT = 640
ROWS = LIVE + STEPS
T = 8
Z = 16
CAP = 2
CHUNKS = ((0, 144), (144, 144), (288, 144), (432, 128))
MESH = pl.DeviceIdType.MESH
F32 = jnp.float32
BF16 = jnp.bfloat16
NT = (((1,), (1,)), ((), ()))


def kernel(
    lens_ref, target_ref, stored_ref, w_ref, bias_ref, gain_ref, dec_ref, resp_ref, keys_ref, values_ref,
    dec_out, learn_out,
    piece, wbuf, xbuf, squares, inverse, acc, projected, attn, kbuf, vbuf, qdec, odec, starts, counts,
    piece_send, piece_recv, sq_send, sq_recv, x_send, x_recv, z_send, z_recv, c_send, c_recv, a_send, a_recv, local_sem,
):
    r, t = lax.axis_index("replica"), lax.axis_index("tensor")
    xl, z, core = r // 32, (r // 2) % Z, r % 2
    a, b = t // 4, t % 4

    def at(xl_, z_, core_, t_):
        return (xl_ * 32 + z_ * 2 + core_, t_)

    def tensor_peer(d):
        return (r, (t + d) % T)

    up, down = at(xl, (z + 1) % Z, core, t), at(xl, (z + Z - 1) % Z, core, t)
    mate = at(xl, z, 1 - core, t)
    y_next, y_prev = (r, a * 4 + (b + 1) % 4), (r, a * 4 + (b + 3) % 4)
    other = (1 - a) * 4
    x_mate = (r, other + b)
    sent = []

    def remote(src, dst, send, recv, device):
        copy = pltpu.make_async_remote_copy(src, dst, send, recv, device_id=device, device_id_type=MESH)
        copy.start()
        sent.append(copy)

    def arrived(dst, recv, send):
        pltpu.make_async_remote_copy(dst, dst, send, recv, device_id=mate, device_id_type=MESH).wait_recv()

    barrier = pltpu.get_barrier_semaphore()
    peers = [tensor_peer(d) for d in range(1, T)]
    peers += [at(1 - xl, z, core, (t + d) % T) for d in range(T)]
    peers += [up, down, mate]
    for peer in peers:
        pl.semaphore_signal(barrier, inc=1, device_id=peer, device_id_type=MESH)

    local = []

    def bring(src, dst):
        copy = pltpu.make_async_copy(src, dst, local_sem.at[len(local)])
        copy.start()
        local.append(copy)

    for f in range(T):
        bring(dec_ref.at[:, f * FEAT : (f + 1) * FEAT], xbuf.at[f, LIVE:ROWS, :])
    bring(w_ref.at[:, pl.ds(pl.multiple_of(t * COLS, 128), COLS)], piece.at[xl * T + t])
    bring(keys_ref, kbuf)
    bring(values_ref, vbuf)

    pl.semaphore_wait(barrier, len(peers))

    for dx in range(2):
        for d in range(T):
            if dx == 0 and d == 0:
                continue
            k = (t + d) % T
            remote(
                w_ref.at[:, pl.ds(pl.multiple_of(k * COLS, 128), COLS)],
                piece.at[xl * T + t],
                piece_send.at[dx, d],
                piece_recv.at[dx, d],
                at((xl + dx) % 2, z, core, k),
            )

    ends, total = [], jnp.int32(0)
    for j in range(DONE):
        total = total + lens_ref[0, j]
        ends.append(total)
    row = lax.broadcasted_iota(jnp.int32, (LIVE, 128), 0)
    source = row
    for j in range(DONE - 1):
        source = source + jnp.where(row >= ends[j], LIMIT - lens_ref[0, j], 0)
    lane = lax.broadcasted_iota(jnp.int32, (LIVE, 128), 1)
    chosen = jnp.concatenate(
        [jnp.where(lane + 128 * i == source, 1.0, 0.0).astype(BF16) for i in range(5)], axis=1
    )
    packed = jnp.dot(chosen, resp_ref[...], preferred_element_type=F32)
    xbuf[t, 0:LIVE, :] = packed.astype(BF16)

    def x_part(f, c):
        return xbuf.at[f, pl.ds(*CHUNKS[c]), :]

    def x_to(kind, f, c, device):
        remote(x_part(f, c), x_part(f, c), x_send.at[kind, c], x_recv.at[kind, c], device)

    def x_from(kind, f, c):
        arrived(x_part(f, c), x_recv.at[kind, c], x_send.at[kind, c])

    for c in range(4):
        x_to(0, t, c, y_next)
        x_to(1, t, c, y_prev)
        x_to(2, t, c, x_mate)

    sq = jnp.concatenate([packed * packed, jnp.zeros((640 - LIVE, FEAT), F32)], axis=0)
    wide = lax.dot_general(
        jnp.ones((8, FEAT), F32), sq, NT, precision=lax.Precision.HIGHEST, preferred_element_type=F32
    )
    sub = lax.broadcasted_iota(jnp.int32, (8, 128), 0)
    dense = jnp.zeros((8, 128), F32)
    for i in range(5):
        dense = jnp.where(sub == i, wide[:, 128 * i : 128 * (i + 1)], dense)
    squares[t] = dense
    for d in range(1, T):
        remote(squares.at[t], squares.at[t], sq_send.at[d], sq_recv.at[d], tensor_peer(d))

    def w_rows(z_, xl_, core_):
        return wbuf.at[pl.ds(pl.multiple_of(xl_ * 2560 + z_ * 160 + core_ * 80, 16), 80), :]

    local[T].wait()
    for dx in range(2):
        for d in range(T):
            if dx or d:
                slot = ((xl + dx) % 2) * T + (t + T - d) % T
                arrived(piece.at[slot], piece_recv.at[dx, d], piece_send.at[dx, d])
    for x_ in range(2):
        block = jnp.concatenate([piece[x_ * T + f].astype(F32) for f in range(T)], axis=0)
        w_rows(z, x_, core)[...] = block.astype(BF16)

    def z_hop(s):
        for x_ in range(2):
            if s < 7 or x_ == 0:
                src = w_rows((z + Z - s) % Z, x_, core)
                remote(src, src, z_send.at[0, s, x_], z_recv.at[0, s, x_], up)
            if s < 7 or x_ == 1:
                src = w_rows((z + s) % Z, x_, core)
                remote(src, src, z_send.at[1, s, x_], z_recv.at[1, s, x_], down)

    def z_step(s):
        for x_ in range(2):
            for way in range(2):
                if s == 8 and x_ != way:
                    continue
                dst = w_rows((z + (s if way else Z - s)) % Z, x_, core)
                arrived(dst, z_recv.at[way, s - 1, x_], z_send.at[way, s - 1, x_])
                if s < 7 or (s == 7 and x_ == way):
                    remote(dst, dst, z_send.at[way, s, x_], z_recv.at[way, s, x_], down if way else up)
                remote(dst, dst, c_send.at[way, s, x_], c_recv.at[way, s, x_], mate)

    def from_mate(s):
        for x_ in range(2):
            for way in range(2):
                if (s == 8 and x_ != way) or (s == 0 and way):
                    continue
                dst = w_rows((z + (s if way else Z - s)) % Z, x_, 1 - core)
                arrived(dst, c_recv.at[way, s, x_], c_send.at[way, s, x_])

    z_hop(0)
    for x_ in range(2):
        src = w_rows(z, x_, core)
        remote(src, src, c_send.at[0, 0, x_], c_recv.at[0, 0, x_], mate)

    for copy in local[:T]:
        copy.wait()
    step_sum = jnp.zeros((STEPS, 1), F32)
    for f in range(T):
        part = xbuf[f, LIVE:ROWS, :].astype(F32)
        step_sum = step_sum + jnp.sum(part * part, axis=1, keepdims=True)
    for d in range(1, T):
        slot = squares.at[(t + T - d) % T]
        arrived(slot, sq_recv.at[d], sq_send.at[d])
    total_sq = squares[0]
    for f in range(1, T):
        total_sq = total_sq + squares[f]
    inv = lax.rsqrt(total_sq * (1.0 / MODEL_WIDTH) + 1e-6)
    for i in range(5):
        inverse[128 * i : 128 * (i + 1), :] = jnp.transpose(jnp.broadcast_to(inv[i : i + 1, :], (128, 128)))
    inverse[LIVE:ROWS, :] = jnp.broadcast_to(lax.rsqrt(step_sum * (1.0 / MODEL_WIDTH) + 1e-6), (STEPS, 128))

    def multiply(f, first=False):
        parts = []
        for i in range(5):
            lanes = slice(128 * i, 128 * (i + 1))
            part = xbuf[f, :, lanes].astype(F32) * inverse[0:ROWS, :]
            parts.append((part * gain_ref[f, :, lanes]).astype(BF16))
        product = jnp.dot(
            jnp.concatenate(parts, axis=1),
            wbuf[pl.ds(pl.multiple_of(f * FEAT, 128), FEAT), :],
            preferred_element_type=F32,
        )
        acc[...] = product if first else acc[...] + product

    projected[ROWS:640, :] = jnp.zeros((640 - ROWS, COLS), BF16)
    slots, begin = [], jnp.int32(0)
    for j in range(DONE):
        earlier = jnp.int32(0)
        for i in range(j):
            earlier = earlier + jnp.where(target_ref[i, 0] == target_ref[j, 0], 1, 0)
        slots.append(target_ref[j, 0] * CAP + earlier)
    for s in range(T * CAP):
        first_row, held = jnp.int32(0), jnp.int32(0)
        for j in range(DONE):
            hit = slots[j] == s
            first_row = first_row + jnp.where(hit, ends[j] - lens_ref[0, j], 0)
            held = held + jnp.where(hit, lens_ref[0, j], 0)
        starts[s] = first_row
        counts[s] = held

    def f_next(side, d=1):
        return side + (b + d) % 4

    own = a * 4

    def own_direct(c):
        x_from(0, f_next(own, 3), c)
        if c < 2:
            x_to(3, f_next(own, 3), c, y_next)
        x_from(1, f_next(own, 1), c)
        if c >= 2:
            x_to(4, f_next(own, 1), c, y_prev)

    def mate_direct(c):
        x_from(2, other + b, c)
        x_to(5, other + b, c, y_next)
        x_to(6, other + b, c, y_prev)

    def mate_relayed(c):
        x_from(5, f_next(other, 3), c)
        if c < 2:
            x_to(7, f_next(other, 3), c, y_next)
        x_from(6, f_next(other, 1), c)
        if c >= 2:
            x_to(8, f_next(other, 1), c, y_prev)

    def far(kind, side):
        for c in range(4):
            x_from(kind if c < 2 else kind + 1, f_next(side, 2), c)

    q, p = z // 4, z % 4
    near = (q + 3 + 2 * (p // 2)) % 4
    opposite = (q + 2) % 4
    wide_side = (q + 1 + 2 * (p // 2)) % 4

    own_direct(0)
    z_step(1)
    own_direct(1)
    mate_direct(0)
    own_direct(2)
    own_direct(3)
    z_step(2)
    mate_direct(1)
    z_step(3)
    mate_direct(2)
    far(3, own)
    for s in range(4):
        from_mate(s)
    multiply(own + q, first=True)
    mate_direct(3)
    z_step(4)
    mate_relayed(0)
    mate_relayed(1)
    z_step(5)
    mate_relayed(2)
    from_mate(4)
    from_mate(5)
    multiply(own + near)
    mate_relayed(3)
    z_step(6)
    z_step(7)
    from_mate(6)
    from_mate(7)
    multiply(own + wide_side)
    far(7, other)
    multiply(other + q)
    multiply(other + near)
    z_step(8)
    multiply(other + wide_side)
    from_mate(8)
    multiply(own + opposite)
    multiply(other + opposite)

    scale = 1.0 / math.sqrt(HEAD_DIM)
    projected[0:ROWS, :] = (acc[...] + bias_ref[...]).astype(BF16)
    at_row = lax.broadcasted_iota(jnp.int32, (128, 128), 0)
    at_col = lax.broadcasted_iota(jnp.int32, (128, 128), 1)
    causal = (at_col <= at_row) & (at_col // LIMIT == at_row // LIMIT)

    def pair(d):
        k = (t + d) % T
        first_row = jnp.where(at_row < LIMIT, starts[CAP * k], starts[CAP * k + 1] - LIMIT)
        wanted = first_row + at_row
        chosen = jnp.concatenate(
            [jnp.where(at_col + 128 * i == wanted, 1.0, 0.0).astype(BF16) for i in range(5)], axis=1
        )
        rows = jnp.dot(chosen, projected[...], preferred_element_type=F32).astype(BF16)
        keys = rows[:, HEADS * HEAD_DIM : (HEADS + 1) * HEAD_DIM]
        vals = rows[:, (HEADS + 1) * HEAD_DIM :]
        held = jnp.where(at_row < LIMIT, counts[2 * k], counts[2 * k + 1] + LIMIT)
        live = at_row < held
        for g in range(HEADS):
            cols = slice(g * HEAD_DIM, (g + 1) * HEAD_DIM)
            scores = lax.dot_general(rows[:, cols], keys, NT, preferred_element_type=F32) * scale
            peak = jnp.max(jnp.where(causal, scores, -jnp.inf), axis=-1, keepdims=True)
            powers = jnp.where(causal, jnp.exp(scores - peak), 0.0)
            probs = (powers / jnp.sum(powers, axis=-1, keepdims=True)).astype(BF16)
            mixed = jnp.dot(probs, vals, preferred_element_type=F32)
            mixed = jnp.where(live, mixed, 0.0).astype(BF16)
            for h in range(CAP):
                attn[CAP * k + h, :, cols] = mixed[h * LIMIT : (h + 1) * LIMIT]

    def outgoing(k):
        return attn.at[pl.ds(CAP * k, CAP), :, :]

    def landing(f):
        return learn_out.at[:, :, pl.ds(pl.multiple_of(f * OUT, 128), OUT)]

    order = (6, 2, 5, 3, 7, 1, 4)
    for d in order:
        pair(d)
        remote(outgoing((t + d) % T), landing(t), a_send.at[d], a_recv.at[d], tensor_peer(d))
    pair(0)
    bring(outgoing(t), landing(t))

    step_rows = projected[LIVE:ROWS, :]
    k_new = step_rows[:, HEADS * HEAD_DIM : (HEADS + 1) * HEAD_DIM].astype(F32)
    v_new = step_rows[:, (HEADS + 1) * HEAD_DIM :].astype(F32)
    qdec[...] = jnp.zeros_like(qdec)
    for g in range(HEADS):
        query = step_rows[:, g * HEAD_DIM : (g + 1) * HEAD_DIM].astype(F32)
        qdec[:, g, :] = query
    odec[:, 0, :] = k_new
    odec[:, 1, :] = v_new
    local[T + 1].wait()
    local[T + 2].wait()
    seen = lax.broadcasted_iota(jnp.int32, (8, CACHE), 1)

    def request(i, carry):
        query = qdec[i]
        fresh = odec[i]
        own_score = jnp.sum(query * fresh[0:1, :], axis=-1, keepdims=True) * scale
        scores = lax.dot_general(query.astype(BF16), kbuf[i], NT, preferred_element_type=F32) * scale
        filled = seen < stored_ref[0, i]
        peak = jnp.maximum(jnp.max(jnp.where(filled, scores, -jnp.inf), axis=-1, keepdims=True), own_score)
        powers = jnp.where(filled, jnp.exp(scores - peak), 0.0)
        own_power = jnp.exp(own_score - peak)
        whole = jnp.sum(powers, axis=-1, keepdims=True) + own_power
        probs = (powers / whole).astype(BF16)
        own_prob = (own_power / whole).astype(BF16).astype(F32)
        mixed = jnp.dot(probs, vbuf[i], preferred_element_type=F32)
        odec[i] = mixed + own_prob * fresh[1:2, :]
        return carry

    lax.fori_loop(0, STEPS, request, 0)
    for g in range(HEADS):
        dec_out[:, g * HEAD_DIM : (g + 1) * HEAD_DIM] = odec[:, g, :].astype(BF16)

    local[-1].wait()
    for d in range(1, T):
        arrived(landing((t + T - d) % T), a_recv.at[d], a_send.at[d])
    for copy in sent:
        copy.wait_send()


def body(
    qkv_weight,
    qkv_bias,
    norm_gain,
    decode_hidden,
    stored_keys,
    stored_values,
    stored_lengths,
    response_hidden,
    response_lengths,
    response_target,
):
    vmem = pl.BlockSpec(memory_space=pltpu.VMEM)
    smem = pl.BlockSpec(memory_space=pltpu.SMEM)
    anywhere = pl.BlockSpec(memory_space=pl.ANY)
    dma = pltpu.SemaphoreType.DMA
    return pl.pallas_call(
        kernel,
        out_shape=(
            jax.ShapeDtypeStruct((STEPS, OUT), BF16),
            jax.ShapeDtypeStruct((CAP, LIMIT, T * OUT), BF16),
        ),
        in_specs=[smem, smem, smem, vmem, vmem, vmem, anywhere, vmem, anywhere, anywhere],
        out_specs=(vmem, anywhere),
        scratch_shapes=[
            pltpu.VMEM((2 * T, 10, COLS), BF16),
            pltpu.VMEM((MODEL_WIDTH, COLS), BF16),
            pltpu.VMEM((T, ROWS, FEAT), BF16),
            pltpu.VMEM((T, 8, 128), F32),
            pltpu.VMEM((640, 128), F32),
            pltpu.VMEM((ROWS, COLS), F32),
            pltpu.VMEM((640, COLS), BF16),
            pltpu.VMEM((T * CAP, LIMIT, OUT), BF16),
            pltpu.VMEM((STEPS, CACHE, HEAD_DIM), BF16),
            pltpu.VMEM((STEPS, CACHE, HEAD_DIM), BF16),
            pltpu.VMEM((STEPS, 8, HEAD_DIM), F32),
            pltpu.VMEM((STEPS, 8, HEAD_DIM), F32),
            pltpu.SMEM((T * CAP,), jnp.int32),
            pltpu.SMEM((T * CAP,), jnp.int32),
            dma((2, T)), dma((2, T)),
            dma((T,)), dma((T,)),
            dma((9, 4)), dma((9, 4)),
            dma((2, 8, 2)), dma((2, 8, 2)),
            dma((2, 9, 2)), dma((2, 9, 2)),
            dma((T,)), dma((T,)),
            dma((T + 4,)),
        ],
        compiler_params=pltpu.CompilerParams(
            collective_id=0, has_side_effects=True, vmem_limit_bytes=56 << 20
        ),
        name="project_and_attend",
    )(
        response_lengths,
        response_target,
        stored_lengths,
        qkv_weight,
        qkv_bias.astype(F32).reshape(1, COLS),
        norm_gain.astype(F32).reshape(T, 1, FEAT),
        decode_hidden,
        response_hidden.reshape(DONE * LIMIT, FEAT),
        stored_keys.reshape(STEPS, CACHE, HEAD_DIM),
        stored_values.reshape(STEPS, CACHE, HEAD_DIM),
    )


def solution(mesh):
    return jax.shard_map(
        body,
        mesh=mesh,
        in_specs=(
            P(("replica", "tensor"), None),
            P("tensor"),
            P(),
            P("replica", None),
            P("replica", "tensor", None, None),
            P("replica", "tensor", None, None),
            P("replica", None),
            P("replica", None, "tensor"),
            P("replica", None),
            P("replica", None),
        ),
        out_specs=(P("replica", "tensor"), P(("replica", "tensor"), None, None)),
        check_vma=False,
    )
```

time: 313 us -> 122 us (0.39)
  waiting for transfers between devices: 234 us -> 0 us
  Pallas kernels: 0 us -> 113 us
  matrix products: 21.8 us -> 0 us
  blocking collectives: 14.8 us -> 0 us
  between operations: 14.3 us -> 0.64 us
  other arithmetic: 11.5 us -> 1.31 us
  starting transfers between devices: 6.51 us -> 0 us
  local copies, waits for them, and re-layouts: 9.97 us -> 6.41 us
    all_gather x2 -> x0, waiting for transfers between devices: 217 us -> none  [the longest x1 121 us: body(): weight_all = lax.all_gather(blocks, 'replica', axis=0, tiled=True)]
    pallas_call x0 -> x1, Pallas kernels: none -> 113 us  [body(): pl.pallas_call(kernel, out_shape=(jax.ShapeDtypeStruct((STEPS, OUT), BF16...]
    dot_general x8 -> x0, matrix products: 21.8 us -> none  [the longest x1 11.8 us: body(): jnp.dot(resp_norm, weight_all, preferred_element_type=jnp.float32)]
    all_to_all x1 -> x0, waiting for transfers between devices: 15.4 us -> none  [body(): lax.all_to_all(sendbuf, 'tensor', split_axis=2, concat_axis=2, tiled=True)]
    all_to_all x1 -> x0, blocking collectives: 14.8 us -> none  [body(): lax.all_to_all(qkv_weight.reshape(rows_local, tensor_count, col_width), '...]
    all_to_all x1 -> x0, starting transfers between devices: 6.43 us -> none  [body(): lax.all_to_all(sendbuf, 'tensor', split_axis=2, concat_axis=2, tiled=True)]
    convert_element_type x4 -> x0, other arithmetic: 5.32 us -> none  [the longest x1 5.3 us: normalize(): (widened * inverse * gain_vec.astype(jnp.float32)).astype(jnp.bfloat16)]
    reduce_sum x5 -> x0, other arithmetic: 5 us -> none  [the longest x2 4.52 us: normalize(): jnp.mean(widened * widened, axis=-1, keepdims=True) + 1e-06]
  transfers between devices with their start and end apart: 3 -> 0, of which waited for: 3 -> 0; matrix products, arithmetic and copies ran while one was open for 6% -> 0% of each run, Pallas kernels for 0% -> 0%
where the time goes in v1:
time: 122 us
  Pallas kernels  113 us (93%)
  local copies, waits for them, and re-layouts  6.41 us (5%)
  other arithmetic  1.31 us (1%)
    pallas_call x1, Pallas kernels, body(): pl.pallas_call(kernel, out_shape=(jax.ShapeDtypeStruct((STEPS, OUT), BF16...  113 us
    unnamed x3, local copies, waits for them, and re-layouts  5.13 us

profile of v1, /device:TPU:1, one launch (start us, length us, event | category | flops | bytes accessed | tf_op | source)
XLA Modules:
  0.0 121.8 jit_solution(4821455797517303229)
XLA Ops:
  0.6 1.3 %reshape.31.bias_ref = f32[1,896]{1,0:T(1,128)} reshape(bf16[896]{0:T(1024)(128)(2,1)} %param.11) | data formatting | bytes 5376 | tf_op jit(solution)/shard_map/reshape | solution.py:442
  1.9 1.3 %copy.12.target_ref = s32[10,1]{1,0:T(8,128)} copy(s32[10,1]{0,1:T(1,128)} %param.19) | data formatting | bytes 80 | tf_op args[9]
  3.2 1.3 %reshape.32 = f32[5120]{0:T(1024)} convert(bf16[5120]{0:T(1024)(128)(2,1)} %param.12) | non-fusion elementwise | flops 5120 | bytes 30720 | tf_op jit(solution)/shard_map/reshape | solution.py:443
  4.6 113.5 %project_and_attend.1 = (bf16[16,640]{1,0:T(8,128)(2,1)}, bf16[2,64,5120]{2,1,0:T(8,128)(2,1)}) custom-call(s32[1,10]{1,0:T(1,128)} %lens_ref.1, s32[10,1]{1,0:T(8,128)} %copy.12.target_ref, s32[1,16]{1,0:T(1,128)} %stored_ref.1, bf16[10,7168]{1,0:T(8,128)(2,1)} %w_ref.1, f32[1,896]{1,0:T(1,128)} %reshape.31.bias_ref, f32[8,1,640]{2,1,0:T(1,128)} %bitcast.7, ...), custom_call_target="tpu_custom_call" | custom-call | tf_op jit(solution)/shard_map/project_and_attend/pallas_call | solution.py:402
  118.0 1.3 %copy.15 = bf16[16,640]{1,0:T(8,128)(2,1)} copy(bf16[16,640]{1,0:T(8,128)(2,1)} %get-tuple-element.4) | data formatting | bytes 40960
  119.4 2.5 %copy.16 = bf16[2,64,5120]{2,1,0:T(8,128)(2,1)} copy(bf16[2,64,5120]{2,1,0:T(8,128)(2,1)} %get-tuple-element.5) | data formatting | bytes 2621440

commit v2 on v1

--- a/solution.py
+++ b/solution.py
@@ -22,6 +22,8 @@
 T = 8
 Z = 16
 CAP = 2
+KEEP = 48
+GROUP = 2
 CHUNKS = ((0, 144), (144, 144), (288, 144), (432, 128))
 MESH = pl.DeviceIdType.MESH
 F32 = jnp.float32
@@ -32,8 +34,8 @@
 def kernel(
     lens_ref, target_ref, stored_ref, w_ref, bias_ref, gain_ref, dec_ref, resp_ref, keys_ref, values_ref,
     dec_out, learn_out,
-    piece, wbuf, xbuf, squares, inverse, acc, projected, attn, kbuf, vbuf, qdec, odec, starts, counts,
-    piece_send, piece_recv, sq_send, sq_recv, x_send, x_recv, z_send, z_recv, c_send, c_recv, a_send, a_recv, local_sem,
+    piece, wbuf, xbuf, squares, inverse, gains, acc, projected, attn, kbuf, vbuf, qdec, odec, starts, counts,
+    piece_send, piece_recv, sq_send, sq_recv, x_send, x_recv, z_send, z_recv, c_send, c_recv, g_send, g_recv, a_send, a_recv, local_sem,
 ):
     r, t = lax.axis_index("replica"), lax.axis_index("tensor")
     xl, z, core = r // 32, (r // 2) % Z, r % 2
@@ -50,6 +52,7 @@
     y_next, y_prev = (r, a * 4 + (b + 1) % 4), (r, a * 4 + (b + 3) % 4)
     other = (1 - a) * 4
     x_mate = (r, other + b)
+    across = at(1 - xl, z, core, t)
     sent = []
 
     def remote(src, dst, send, recv, device):
@@ -124,91 +127,113 @@
         x_to(1, t, c, y_prev)
         x_to(2, t, c, x_mate)
 
-    sq = jnp.concatenate([packed * packed, jnp.zeros((640 - LIVE, FEAT), F32)], axis=0)
-    wide = lax.dot_general(
-        jnp.ones((8, FEAT), F32), sq, NT, precision=lax.Precision.HIGHEST, preferred_element_type=F32
+    spans = ((KEEP, 80 - KEEP), (0, KEEP), (0, KEEP), (KEEP, 80 - KEEP))
+
+    def w_part(side, way, s, part, core_):
+        first, count = spans[part]
+        z_ = (z + (s if way else Z - s)) % Z
+        return wbuf.at[pl.ds(pl.multiple_of(side * 2560 + z_ * 160 + core_ * 80 + first, 16), count), :]
+
+    def w_rows(way, s, part, core_):
+        return w_part(1 - xl if part > 1 else xl, way, s, part, core_)
+
+    def last_way(part):
+        return 1 if part == 2 else 0
+
+    def z_hop(way, s, part):
+        rows = w_rows(way, s, part, core)
+        remote(rows, rows, z_send.at[way, s, part], z_recv.at[way, s, part], down if way else up)
+
+    def to_mate(way, s, part):
+        rows = w_rows(way, s, part, core)
+        remote(rows, rows, c_send.at[way, s, part], c_recv.at[way, s, part], mate)
+
+    def z_step(s):
+        for part in range(3):
+            for way in range(2):
+                if s == 8 and last_way(part) != way:
+                    continue
+                rows = w_rows(way, s, part, core)
+                arrived(rows, z_recv.at[way, s - 1, part], z_send.at[way, s - 1, part])
+                if s < 7 or (s == 7 and last_way(part) == way):
+                    z_hop(way, s, part)
+                if part == 0:
+                    remote(rows, rows, g_send.at[way, s], g_recv.at[way, s], across)
+                to_mate(way, s, part)
+
+    def x_step(s):
+        for way in range(2):
+            if s == 8 and way:
+                continue
+            arrived(w_rows(way, s, 3, core), g_recv.at[way, s], g_send.at[way, s])
+            to_mate(way, s, 3)
+
+    def from_mate(s):
+        for part in range(4):
+            for way in range(2):
+                if (s == 8 and last_way(part) != way) or (s == 0 and way):
+                    continue
+                arrived(w_rows(way, s, part, 1 - core), c_recv.at[way, s, part], c_send.at[way, s, part])
+
+    def start_ring():
+        local[T].wait()
+        for dx in range(2):
+            for d in range(T):
+                if dx or d:
+                    slot = ((xl + dx) % 2) * T + (t + T - d) % T
+                    arrived(piece.at[slot], piece_recv.at[dx, d], piece_send.at[dx, d])
+        for half in range(2):
+            side = 1 - xl if half else xl
+            block = jnp.concatenate([piece[side * T + f].astype(F32) for f in range(T)], axis=0)
+            wbuf[pl.ds(pl.multiple_of(side * 2560 + z * 160 + core * 80, 16), 80), :] = block.astype(BF16)
+            for part in range(2 * half, 2 + half):
+                for way in range(2):
+                    z_hop(way, 0, part)
+        for part in range(4):
+            to_mate(0, 0, part)
+
+    start_ring()
+
+    sums = jnp.sum(packed * packed, axis=1, keepdims=True)
+    sums = jnp.concatenate([jnp.broadcast_to(sums, (LIVE, 128)), jnp.zeros((640 - LIVE, 128), F32)], axis=0)
+    dense = jnp.concatenate(
+        [jnp.transpose(sums[128 * i : 128 * (i + 1)])[0:1] for i in range(5)] + [jnp.zeros((3, 128), F32)], axis=0
     )
-    sub = lax.broadcasted_iota(jnp.int32, (8, 128), 0)
-    dense = jnp.zeros((8, 128), F32)
-    for i in range(5):
-        dense = jnp.where(sub == i, wide[:, 128 * i : 128 * (i + 1)], dense)
     squares[t] = dense
     for d in range(1, T):
         remote(squares.at[t], squares.at[t], sq_send.at[d], sq_recv.at[d], tensor_peer(d))
-
-    def w_rows(z_, xl_, core_):
-        return wbuf.at[pl.ds(pl.multiple_of(xl_ * 2560 + z_ * 160 + core_ * 80, 16), 80), :]
-
-    local[T].wait()
-    for dx in range(2):
-        for d in range(T):
-            if dx or d:
-                slot = ((xl + dx) % 2) * T + (t + T - d) % T
-                arrived(piece.at[slot], piece_recv.at[dx, d], piece_send.at[dx, d])
-    for x_ in range(2):
-        block = jnp.concatenate([piece[x_ * T + f].astype(F32) for f in range(T)], axis=0)
-        w_rows(z, x_, core)[...] = block.astype(BF16)
-
-    def z_hop(s):
-        for x_ in range(2):
-            if s < 7 or x_ == 0:
-                src = w_rows((z + Z - s) % Z, x_, core)
-                remote(src, src, z_send.at[0, s, x_], z_recv.at[0, s, x_], up)
-            if s < 7 or x_ == 1:
-                src = w_rows((z + s) % Z, x_, core)
-                remote(src, src, z_send.at[1, s, x_], z_recv.at[1, s, x_], down)
-
-    def z_step(s):
-        for x_ in range(2):
-            for way in range(2):
-                if s == 8 and x_ != way:
-                    continue
-                dst = w_rows((z + (s if way else Z - s)) % Z, x_, core)
-                arrived(dst, z_recv.at[way, s - 1, x_], z_send.at[way, s - 1, x_])
-                if s < 7 or (s == 7 and x_ == way):
-                    remote(dst, dst, z_send.at[way, s, x_], z_recv.at[way, s, x_], down if way else up)
-                remote(dst, dst, c_send.at[way, s, x_], c_recv.at[way, s, x_], mate)
-
-    def from_mate(s):
-        for x_ in range(2):
-            for way in range(2):
-                if (s == 8 and x_ != way) or (s == 0 and way):
-                    continue
-                dst = w_rows((z + (s if way else Z - s)) % Z, x_, 1 - core)
-                arrived(dst, c_recv.at[way, s, x_], c_send.at[way, s, x_])
-
-    z_hop(0)
-    for x_ in range(2):
-        src = w_rows(z, x_, core)
-        remote(src, src, c_send.at[0, 0, x_], c_recv.at[0, 0, x_], mate)
-
-    for copy in local[:T]:
-        copy.wait()
-    step_sum = jnp.zeros((STEPS, 1), F32)
     for f in range(T):
-        part = xbuf[f, LIVE:ROWS, :].astype(F32)
-        step_sum = step_sum + jnp.sum(part * part, axis=1, keepdims=True)
-    for d in range(1, T):
-        slot = squares.at[(t + T - d) % T]
-        arrived(slot, sq_recv.at[d], sq_send.at[d])
-    total_sq = squares[0]
-    for f in range(1, T):
-        total_sq = total_sq + squares[f]
-    inv = lax.rsqrt(total_sq * (1.0 / MODEL_WIDTH) + 1e-6)
-    for i in range(5):
-        inverse[128 * i : 128 * (i + 1), :] = jnp.transpose(jnp.broadcast_to(inv[i : i + 1, :], (128, 128)))
-    inverse[LIVE:ROWS, :] = jnp.broadcast_to(lax.rsqrt(step_sum * (1.0 / MODEL_WIDTH) + 1e-6), (STEPS, 128))
-
-    def multiply(f, first=False):
+        gain = gain_ref[f * FEAT : (f + 1) * FEAT].astype(F32).reshape(1, FEAT)
+        gains[f] = jnp.broadcast_to(gain, (8, FEAT))
+
+    def norms():
+        for copy in local[:T]:
+            copy.wait()
+        step_sum = jnp.zeros((STEPS, 1), F32)
+        for f in range(T):
+            part = xbuf[f, LIVE:ROWS, :].astype(F32)
+            step_sum = step_sum + jnp.sum(part * part, axis=1, keepdims=True)
+        for d in range(1, T):
+            slot = squares.at[(t + T - d) % T]
+            arrived(slot, sq_recv.at[d], sq_send.at[d])
+        total_sq = squares[0]
+        for f in range(1, T):
+            total_sq = total_sq + squares[f]
+        inv = lax.rsqrt(total_sq * (1.0 / MODEL_WIDTH) + 1e-6)
+        for i in range(5):
+            inverse[128 * i : 128 * (i + 1), :] = jnp.transpose(jnp.broadcast_to(inv[i : i + 1, :], (128, 128)))
+        inverse[LIVE:ROWS, :] = jnp.broadcast_to(lax.rsqrt(step_sum * (1.0 / MODEL_WIDTH) + 1e-6), (STEPS, 128))
+
+    def multiply(*blocks, first=False):
         parts = []
-        for i in range(5):
-            lanes = slice(128 * i, 128 * (i + 1))
-            part = xbuf[f, :, lanes].astype(F32) * inverse[0:ROWS, :]
-            parts.append((part * gain_ref[f, :, lanes]).astype(BF16))
+        for f in blocks:
+            for i in range(5):
+                lanes = slice(128 * i, 128 * (i + 1))
+                part = xbuf[f, :, lanes].astype(F32) * inverse[0:ROWS, :]
+                parts.append((part * gains[f, 0:1, lanes]).astype(BF16))
+        weights = [wbuf[pl.ds(pl.multiple_of(f * FEAT, 128), FEAT), :] for f in blocks]
         product = jnp.dot(
-            jnp.concatenate(parts, axis=1),
-            wbuf[pl.ds(pl.multiple_of(f * FEAT, 128), FEAT), :],
-            preferred_element_type=F32,
+            jnp.concatenate(parts, axis=1), jnp.concatenate(weights, axis=0), preferred_element_type=F32
         )
         acc[...] = product if first else acc[...] + product
 
@@ -217,8 +242,8 @@
     for j in range(DONE):
         earlier = jnp.int32(0)
         for i in range(j):
-            earlier = earlier + jnp.where(target_ref[i, 0] == target_ref[j, 0], 1, 0)
-        slots.append(target_ref[j, 0] * CAP + earlier)
+            earlier = earlier + jnp.where(target_ref[0, i] == target_ref[0, j], 1, 0)
+        slots.append(target_ref[0, j] * CAP + earlier)
     for s in range(T * CAP):
         first_row, held = jnp.int32(0), jnp.int32(0)
         for j in range(DONE):
@@ -264,57 +289,72 @@
     wide_side = (q + 1 + 2 * (p // 2)) % 4
 
     own_direct(0)
+    mate_direct(0)
     z_step(1)
     own_direct(1)
-    mate_direct(0)
+    mate_direct(1)
+    z_step(2)
+    x_step(1)
     own_direct(2)
+    mate_direct(2)
+    z_step(3)
+    x_step(2)
     own_direct(3)
-    z_step(2)
-    mate_direct(1)
-    z_step(3)
-    mate_direct(2)
+    mate_direct(3)
+    z_step(4)
+    x_step(3)
+    norms()
     far(3, own)
+    mate_relayed(0)
     for s in range(4):
         from_mate(s)
+    z_step(5)
+    x_step(4)
+    mate_relayed(1)
     multiply(own + q, first=True)
-    mate_direct(3)
-    z_step(4)
-    mate_relayed(0)
-    mate_relayed(1)
-    z_step(5)
+    z_step(6)
+    x_step(5)
     mate_relayed(2)
     from_mate(4)
     from_mate(5)
     multiply(own + near)
+    z_step(7)
+    x_step(6)
     mate_relayed(3)
-    z_step(6)
-    z_step(7)
+    z_step(8)
+    x_step(7)
     from_mate(6)
     from_mate(7)
     multiply(own + wide_side)
+    x_step(8)
     far(7, other)
-    multiply(other + q)
-    multiply(other + near)
-    z_step(8)
-    multiply(other + wide_side)
+    multiply(other + q, other + near, other + wide_side)
     from_mate(8)
-    multiply(own + opposite)
-    multiply(other + opposite)
+    multiply(own + opposite, other + opposite)
 
     scale = 1.0 / math.sqrt(HEAD_DIM)
-    projected[0:ROWS, :] = (acc[...] + bias_ref[...]).astype(BF16)
+    projected[0:ROWS, :] = (acc[...] + bias_ref[...].astype(F32).reshape(1, COLS)).astype(BF16)
     at_row = lax.broadcasted_iota(jnp.int32, (128, 128), 0)
     at_col = lax.broadcasted_iota(jnp.int32, (128, 128), 1)
     causal = (at_col <= at_row) & (at_col // LIMIT == at_row // LIMIT)
 
-    def pair(d):
-        k = (t + d) % T
-        first_row = jnp.where(at_row < LIMIT, starts[CAP * k], starts[CAP * k + 1] - LIMIT)
-        wanted = first_row + at_row
-        chosen = jnp.concatenate(
-            [jnp.where(at_col + 128 * i == wanted, 1.0, 0.0).astype(BF16) for i in range(5)], axis=1
-        )
-        rows = jnp.dot(chosen, projected[...], preferred_element_type=F32).astype(BF16)
+    def learner(dx, dy):
+        return (a + dx) % 2 * 4 + (b + dy) % 4
+
+    def spread(targets):
+        picks = []
+        for k in targets:
+            first_row = jnp.where(at_row < LIMIT, starts[CAP * k], starts[CAP * k + 1] - LIMIT)
+            wanted = first_row + at_row
+            picks.append(
+                jnp.concatenate(
+                    [jnp.where(at_col + 128 * i == wanted, 1.0, 0.0).astype(BF16) for i in range(5)], axis=1
+                )
+            )
+        picked = jnp.dot(jnp.concatenate(picks, axis=0), projected[...], preferred_element_type=F32)
+        return [picked[128 * i : 128 * (i + 1)].astype(BF16) for i in range(len(targets))]
+
+    def pair(k, rows):
         keys = rows[:, HEADS * HEAD_DIM : (HEADS + 1) * HEAD_DIM]
         vals = rows[:, (HEADS + 1) * HEAD_DIM :]
         held = jnp.where(at_row < LIMIT, counts[2 * k], counts[2 * k + 1] + LIMIT)
@@ -322,8 +362,8 @@
         for g in range(HEADS):
             cols = slice(g * HEAD_DIM, (g + 1) * HEAD_DIM)
             scores = lax.dot_general(rows[:, cols], keys, NT, preferred_element_type=F32) * scale
-            peak = jnp.max(jnp.where(causal, scores, -jnp.inf), axis=-1, keepdims=True)
-            powers = jnp.where(causal, jnp.exp(scores - peak), 0.0)
+            scores = jnp.where(causal, scores, -jnp.inf)
+            powers = jnp.exp(scores - jnp.max(scores, axis=-1, keepdims=True))
             probs = (powers / jnp.sum(powers, axis=-1, keepdims=True)).astype(BF16)
             mixed = jnp.dot(probs, vals, preferred_element_type=F32)
             mixed = jnp.where(live, mixed, 0.0).astype(BF16)
@@ -336,12 +376,16 @@
     def landing(f):
         return learn_out.at[:, :, pl.ds(pl.multiple_of(f * OUT, 128), OUT)]
 
-    order = (6, 2, 5, 3, 7, 1, 4)
-    for d in order:
-        pair(d)
-        remote(outgoing((t + d) % T), landing(t), a_send.at[d], a_recv.at[d], tensor_peer(d))
-    pair(0)
-    bring(outgoing(t), landing(t))
+    order = ((1, 2), (1, 0), (1, 1), (1, 3), (0, 2), (0, 1), (0, 3))
+    targets = [learner(*step) for step in order] + [t]
+    for n, k in enumerate(targets):
+        if n % GROUP == 0:
+            spreads = spread(targets[n : n + GROUP])
+        pair(k, spreads[n % GROUP])
+        if n < len(order):
+            remote(outgoing(k), landing(t), a_send.at[n], a_recv.at[n], (r, k))
+        else:
+            bring(outgoing(t), landing(t))
 
     step_rows = projected[LIVE:ROWS, :]
     k_new = step_rows[:, HEADS * HEAD_DIM : (HEADS + 1) * HEAD_DIM].astype(F32)
@@ -372,15 +416,33 @@
         odec[i] = mixed + own_prob * fresh[1:2, :]
         return carry
 
-    lax.fori_loop(0, STEPS, request, 0)
+    lax.fori_loop(0, STEPS, request, 0, unroll=4)
     for g in range(HEADS):
         dec_out[:, g * HEAD_DIM : (g + 1) * HEAD_DIM] = odec[:, g, :].astype(BF16)
 
     local[-1].wait()
-    for d in range(1, T):
-        arrived(landing((t + T - d) % T), a_recv.at[d], a_send.at[d])
+    for n, (dx, dy) in enumerate(order):
+        arrived(landing(learner(dx, 4 - dy)), a_recv.at[n], a_send.at[n])
     for copy in sent:
         copy.wait_send()
+
+
+def hand_over(step_in, learner_in, step_out, learner_out, step_buf, buf, sem):
+    def learner_part(ref, i):
+        return ref.at[i // 4, (i % 4) * 16 : (i % 4 + 1) * 16, :]
+
+    n = CAP * 4
+    copies = [pltpu.make_async_copy(learner_part(learner_in, i), buf.at[i], sem.at[i]) for i in range(n)]
+    copies.append(pltpu.make_async_copy(step_in, step_buf, sem.at[n]))
+    outs = [pltpu.make_async_copy(buf.at[i], learner_part(learner_out, i), sem.at[n + 1 + i]) for i in range(n)]
+    outs.append(pltpu.make_async_copy(step_buf, step_out, sem.at[2 * n + 1]))
+    for copy in copies:
+        copy.start()
+    for copy, out in zip(copies, outs):
+        copy.wait()
+        out.start()
+    for out in outs:
+        out.wait()
 
 
 def body(
@@ -399,7 +461,7 @@
     smem = pl.BlockSpec(memory_space=pltpu.SMEM)
     anywhere = pl.BlockSpec(memory_space=pl.ANY)
     dma = pltpu.SemaphoreType.DMA
-    return pl.pallas_call(
+    step, learner = pl.pallas_call(
         kernel,
         out_shape=(
             jax.ShapeDtypeStruct((STEPS, OUT), BF16),
@@ -413,6 +475,7 @@
             pltpu.VMEM((T, ROWS, FEAT), BF16),
             pltpu.VMEM((T, 8, 128), F32),
             pltpu.VMEM((640, 128), F32),
+            pltpu.VMEM((T, 8, FEAT), F32),
             pltpu.VMEM((ROWS, COLS), F32),
             pltpu.VMEM((640, COLS), BF16),
             pltpu.VMEM((T * CAP, LIMIT, OUT), BF16),
@@ -425,8 +488,9 @@
             dma((2, T)), dma((2, T)),
             dma((T,)), dma((T,)),
             dma((9, 4)), dma((9, 4)),
-            dma((2, 8, 2)), dma((2, 8, 2)),
-            dma((2, 9, 2)), dma((2, 9, 2)),
+            dma((2, 8, 3)), dma((2, 8, 3)),
+            dma((2, 9, 4)), dma((2, 9, 4)),
+            dma((2, 9)), dma((2, 9)),
             dma((T,)), dma((T,)),
             dma((T + 4,)),
         ],
@@ -436,16 +500,31 @@
         name="project_and_attend",
     )(
         response_lengths,
-        response_target,
+        response_target.reshape(1, DONE),
         stored_lengths,
         qkv_weight,
-        qkv_bias.astype(F32).reshape(1, COLS),
-        norm_gain.astype(F32).reshape(T, 1, FEAT),
+        qkv_bias,
+        norm_gain,
         decode_hidden,
         response_hidden.reshape(DONE * LIMIT, FEAT),
         stored_keys.reshape(STEPS, CACHE, HEAD_DIM),
         stored_values.reshape(STEPS, CACHE, HEAD_DIM),
     )
+    return pl.pallas_call(
+        hand_over,
+        out_shape=(
+            jax.ShapeDtypeStruct(step.shape, BF16),
+            jax.ShapeDtypeStruct(learner.shape, BF16),
+        ),
+        in_specs=[anywhere, anywhere],
+        out_specs=(anywhere, anywhere),
+        scratch_shapes=[
+            pltpu.VMEM(step.shape, BF16),
+            pltpu.VMEM((CAP * 4, 16, T * OUT), BF16),
+            dma((2 + CAP * 8,)),
+        ],
+        name="hand_over",
+    )(step, learner)
 
 
 def solution(mesh):

time: 122 us -> 111 us (0.910)
  local copies, waits for them, and re-layouts: 6.41 us -> 0 us
  Pallas kernels: 113 us -> 110 us
  other arithmetic: 1.31 us -> 0 us
    pallas_call x1, Pallas kernels: 113 us -> 108 us  [body(): pl.pallas_call(kernel, out_shape=(jax.ShapeDtypeStruct((STEPS, OUT), BF16...]
    unnamed x3 -> x0, local copies, waits for them, and re-layouts: 5.13 us -> none
    pallas_call x0 -> x1, Pallas kernels: none -> 2.23 us  [body(): pl.pallas_call(hand_over, out_shape=(jax.ShapeDtypeStruct(step.shape, BF1...]
    reshape x1 -> x0, other arithmetic: 1.31 us -> none  [body(): norm_gain.astype(F32).reshape(T, 1, FEAT)]
    reshape x1 -> x0, local copies, waits for them, and re-layouts: 1.28 us -> none  [body(): qkv_bias.astype(F32).reshape(1, COLS)]
where the time goes in v2:
time: 111 us
  Pallas kernels  110 us (99%)
    pallas_call x1, Pallas kernels, body(): pl.pallas_call(kernel, out_shape=(jax.ShapeDtypeStruct((STEPS, OUT), BF16...  108 us
    pallas_call x1, Pallas kernels, body(): pl.pallas_call(hand_over, out_shape=(jax.ShapeDtypeStruct(step.shape, BF1...  2.23 us

profile of v2, /device:TPU:1, one launch (start us, length us, event | category | flops | bytes accessed | tf_op | source)
XLA Modules:
  0.0 110.9 jit_solution(7302039801268855338)
XLA Ops:
  0.6 107.9 %project_and_attend.1 = (bf16[16,640]{1,0:T(8,128)(2,1)}, bf16[2,64,5120]{2,1,0:T(8,128)(2,1)}) custom-call(s32[1,10]{1,0:T(1,128)} %lens_ref.1, s32[1,10]{1,0:T(1,128)} %bitcast.7, s32[1,16]{1,0:T(1,128)} %stored_ref.1, bf16[10,7168]{1,0:T(8,128)(2,1)} %w_ref.1, bf16[896]{0:T(1024)(128)(2,1)} %bias_ref.1, bf16[5120]{0:T(1024)(128)(2,1)} %gain_ref.1, ...), custom_call_target="tpu_custom_call" | custom-call | tf_op jit(solution)/shard_map/project_and_attend/pallas_call | solution.py:464
  108.6 2.2 %hand_over.1 = (bf16[16,640]{1,0:T(8,128)(2,1)}, bf16[2,64,5120]{2,1,0:T(8,128)(2,1)}) custom-call(bf16[16,640]{1,0:T(8,128)(2,1)} %get-tuple-element.4.step_in, bf16[2,64,5120]{2,1,0:T(8,128)(2,1)} %get-tuple-element.5.learner_in), custom_call_target="tpu_custom_call" | custom-call | tf_op jit(solution)/shard_map/hand_over/pallas_call | solution.py:513

commit v3 on v2

--- a/solution.py
+++ b/solution.py
@@ -22,7 +22,7 @@
 T = 8
 Z = 16
 CAP = 2
-KEEP = 48
+KEEP = 32
 GROUP = 2
 CHUNKS = ((0, 144), (144, 144), (288, 144), (432, 128))
 MESH = pl.DeviceIdType.MESH
@@ -294,43 +294,43 @@
     own_direct(1)
     mate_direct(1)
     z_step(2)
-    x_step(1)
     own_direct(2)
     mate_direct(2)
+    x_step(1)
     z_step(3)
-    x_step(2)
     own_direct(3)
     mate_direct(3)
+    x_step(2)
     z_step(4)
     x_step(3)
     norms()
+    z_step(5)
+    mate_relayed(0)
+    x_step(4)
     far(3, own)
-    mate_relayed(0)
     for s in range(4):
         from_mate(s)
-    z_step(5)
-    x_step(4)
-    mate_relayed(1)
     multiply(own + q, first=True)
     z_step(6)
+    mate_relayed(1)
+    mate_relayed(2)
     x_step(5)
-    mate_relayed(2)
     from_mate(4)
+    z_step(7)
+    mate_relayed(3)
+    x_step(6)
     from_mate(5)
     multiply(own + near)
-    z_step(7)
-    x_step(6)
-    mate_relayed(3)
     z_step(8)
     x_step(7)
     from_mate(6)
     from_mate(7)
+    x_step(8)
     multiply(own + wide_side)
-    x_step(8)
+    from_mate(8)
+    multiply(own + opposite)
     far(7, other)
-    multiply(other + q, other + near, other + wide_side)
-    from_mate(8)
-    multiply(own + opposite, other + opposite)
+    multiply(other + q, other + near, other + wide_side, other + opposite)
 
     scale = 1.0 / math.sqrt(HEAD_DIM)
     projected[0:ROWS, :] = (acc[...] + bias_ref[...].astype(F32).reshape(1, COLS)).astype(BF16)
@@ -376,7 +376,7 @@
     def landing(f):
         return learn_out.at[:, :, pl.ds(pl.multiple_of(f * OUT, 128), OUT)]
 
-    order = ((1, 2), (1, 0), (1, 1), (1, 3), (0, 2), (0, 1), (0, 3))
+    order = ((1, 2), (0, 2), (1, 1), (0, 1), (1, 3), (1, 0), (0, 3))
     targets = [learner(*step) for step in order] + [t]
     for n, k in enumerate(targets):
         if n % GROUP == 0:

time: 111 us -> 105 us (0.946)
  Pallas kernels: 110 us -> 104 us
    pallas_call x1, Pallas kernels: 108 us -> 102 us  [body(): pl.pallas_call(kernel, out_shape=(jax.ShapeDtypeStruct((STEPS, OUT), BF16...]
where the time goes in v3:
time: 105 us
  Pallas kernels  104 us (99%)
    pallas_call x1, Pallas kernels, body(): pl.pallas_call(kernel, out_shape=(jax.ShapeDtypeStruct((STEPS, OUT), BF16...  102 us
    pallas_call x1, Pallas kernels, body(): pl.pallas_call(hand_over, out_shape=(jax.ShapeDtypeStruct(step.shape, BF1...  2.23 us

profile of v3, /device:TPU:1, one launch (start us, length us, event | category | flops | bytes accessed | tf_op | source)
XLA Modules:
  0.0 104.9 jit_solution(7018578879194000664)
XLA Ops:
  0.6 101.8 %project_and_attend.1 = (bf16[16,640]{1,0:T(8,128)(2,1)}, bf16[2,64,5120]{2,1,0:T(8,128)(2,1)}) custom-call(s32[1,10]{1,0:T(1,128)} %lens_ref.1, s32[1,10]{1,0:T(1,128)} %bitcast.7, s32[1,16]{1,0:T(1,128)} %stored_ref.1, bf16[10,7168]{1,0:T(8,128)(2,1)} %w_ref.1, bf16[896]{0:T(1024)(128)(2,1)} %bias_ref.1, bf16[5120]{0:T(1024)(128)(2,1)} %gain_ref.1, ...), custom_call_target="tpu_custom_call" | custom-call | tf_op jit(solution)/shard_map/project_and_attend/pallas_call | solution.py:464
  102.5 2.2 %hand_over.1 = (bf16[16,640]{1,0:T(8,128)(2,1)}, bf16[2,64,5120]{2,1,0:T(8,128)(2,1)}) custom-call(bf16[16,640]{1,0:T(8,128)(2,1)} %get-tuple-element.4.step_in, bf16[2,64,5120]{2,1,0:T(8,128)(2,1)} %get-tuple-element.5.learner_in), custom_call_target="tpu_custom_call" | custom-call | tf_op jit(solution)/shard_map/hand_over/pallas_call | solution.py:513

commit v4 on v3

--- a/solution.py
+++ b/solution.py
@@ -287,6 +287,14 @@
     near = (q + 3 + 2 * (p // 2)) % 4
     opposite = (q + 2) % 4
     wide_side = (q + 1 + 2 * (p // 2)) % 4
+
+    def early(f):
+        return ((f + 2 - b + 4) % 4 + 3) // 4
+
+    keep = early(q)
+    first_other, left = near + (q - near) * keep, q + (near - q) * keep
+    keep = early(left)
+    second_other, third_other = wide_side + (left - wide_side) * keep, left + (wide_side - left) * keep
 
     own_direct(0)
     mate_direct(0)
@@ -320,17 +328,17 @@
     mate_relayed(3)
     x_step(6)
     from_mate(5)
-    multiply(own + near)
+    multiply(own + near, other + first_other)
     z_step(8)
     x_step(7)
     from_mate(6)
     from_mate(7)
     x_step(8)
-    multiply(own + wide_side)
+    multiply(own + wide_side, other + second_other)
     from_mate(8)
     multiply(own + opposite)
     far(7, other)
-    multiply(other + q, other + near, other + wide_side, other + opposite)
+    multiply(other + third_other, other + opposite)
 
     scale = 1.0 / math.sqrt(HEAD_DIM)
     projected[0:ROWS, :] = (acc[...] + bias_ref[...].astype(F32).reshape(1, COLS)).astype(BF16)

time: 105 us -> 104 us (level)
    pallas_call x1, Pallas kernels: 102 us -> 100 us  [body(): pl.pallas_call(kernel, out_shape=(jax.ShapeDtypeStruct((STEPS, OUT), BF16...]
where the time goes in v4:
time: 104 us; the launch traced here: 103 us
  Pallas kernels  103 us (99%)
    pallas_call x1, Pallas kernels, body(): pl.pallas_call(kernel, out_shape=(jax.ShapeDtypeStruct((STEPS, OUT), BF16...  100 us
    pallas_call x1, Pallas kernels, body(): pl.pallas_call(hand_over, out_shape=(jax.ShapeDtypeStruct(step.shape, BF1...  2.23 us

profile of v4, /device:TPU:1, one launch (start us, length us, event | category | flops | bytes accessed | tf_op | source)
XLA Modules:
  0.0 103.5 jit_solution(10967588122452980109)
XLA Ops:
  0.6 100.5 %project_and_attend.1 = (bf16[16,640]{1,0:T(8,128)(2,1)}, bf16[2,64,5120]{2,1,0:T(8,128)(2,1)}) custom-call(s32[1,10]{1,0:T(1,128)} %lens_ref.1, s32[1,10]{1,0:T(1,128)} %bitcast.7, s32[1,16]{1,0:T(1,128)} %stored_ref.1, bf16[10,7168]{1,0:T(8,128)(2,1)} %w_ref.1, bf16[896]{0:T(1024)(128)(2,1)} %bias_ref.1, bf16[5120]{0:T(1024)(128)(2,1)} %gain_ref.1, ...), custom_call_target="tpu_custom_call" | custom-call | tf_op jit(solution)/shard_map/project_and_attend/pallas_call | solution.py:472
  101.1 2.2 %hand_over.1 = (bf16[16,640]{1,0:T(8,128)(2,1)}, bf16[2,64,5120]{2,1,0:T(8,128)(2,1)}) custom-call(bf16[16,640]{1,0:T(8,128)(2,1)} %get-tuple-element.4.step_in, bf16[2,64,5120]{2,1,0:T(8,128)(2,1)} %get-tuple-element.5.learner_in), custom_call_target="tpu_custom_call" | custom-call | tf_op jit(solution)/shard_map/hand_over/pallas_call | solution.py:521
